TPU v7x, 256 devices: a whole 4x4x8 slice. The times are simulated.
256 devices in a mesh: row: 8 (over x, core), col: 32 (over y, z).
Axes of the slice: x: 4, y: 4, z: 8, core: 2. Of those that a mesh axis runs over, the one named last changes fastest.
Arguments:
- deflation: bfloat16 [16, 256, 16, 3072], P('row', 'col'), may hold values from 0 to 0.019897461
- coefficient: float32 [16, 256, 16], P('row', 'col'), may hold values from 1 to 10
- gradients: bfloat16 [3, 64, 64], replicated, may hold values from -0.75 to 0.75
- x_penalty: float32 [24, 256, 16], P('row', 'col'), may hold values from 1 to 10, as said below
- y_penalty: float32 [16, 288, 16], P('row', 'col'), may hold values from 1 to 10, as said below
- z_penalty: float32 [16, 256, 17], P('row', 'col'), may hold values from 1 to 10
- coarse_order: int32 [1024], replicated, may hold values from 0 to 1023, as said below
Outputs:
- coarse_blocks: float32 [1024, 7, 2304], P(('row', 'col'))
- panel: float32 [1024, 48, 528], P(('row', 'col'))
Inputs may be any that keep to these rules, and one draw needn't show every extreme that they name: `coarse_order`: each subdomain number appears once; subdomains with consecutive coarse numbers are mostly neighbours along the third or second dimension. `x_penalty`: row i * 3 + 2 equals row (i + 1) * 3: a face between two devices' blocks is held by both. `y_penalty`: column j * 9 + 8 equals column (j + 1) * 9: a face between two devices' blocks is held by both.
All inputs are finite; a program needn't handle non-finite values.
Results may differ from a plain program's by a relative error of at most 0.00044.
Values may be sent and summed in bfloat16 or wider, within the bound.
No kernel may reach another device: no remote copies, remote signals or barrier semaphores. Data moves between devices by JAX's collectives and lax.ppermute only.
A program may use at most 128 MiB of HBM per device.

v0:
```python
import jax
import jax.numpy as jnp
from jax import lax
from jax.experimental import pallas as pl
from jax.experimental.pallas import tpu as pltpu
from jax.sharding import PartitionSpec as P

NV = 48
SUB_DEV = 4
PB = 11
SUBS = 1024
N_ROW = 8
N_COL = 32


LINE_WEIGHTS = (1.0 / 6.0, 5.0 / 6.0, 5.0 / 6.0, 1.0 / 6.0)
COEF, XPEN, YPEN, ZPEN = 0, 16, 40, 58


def fetch(tiles, start, target):
    lane = lax.broadcasted_iota(jnp.int32, tiles[0].shape, 1)
    tile, offset = start // 128, start % 128
    shift = (target - offset) % 128
    first = pltpu.roll(tiles[tile], shift, 1) if shift else tiles[tile]
    if offset + NV <= 128:
        return first
    second = pltpu.roll(tiles[tile + 1], shift, 1) if shift else tiles[tile + 1]
    return jnp.where(lane >= target + 128 - offset, second, first)


def paired(even, odd, start):
    lane = lax.broadcasted_iota(jnp.int32, even[0].shape, 1)
    return jnp.where(lane < 64, fetch(even, start, 0), fetch(odd, start, 64))


def lane_tiles(values):
    wide = values.astype(jnp.float32)
    return [wide[:, 128 * t : 128 * t + 128] for t in range(wide.shape[1] // 128)]


def gram(left, right):
    return lax.dot_general(left, right, (((0,), (0,)), ((), ())), preferred_element_type=jnp.float32)


def assemble_kernel(deflation, gradients, coefficient, x_penalty, y_penalty, z_penalty, main, own_x, own_y, roots_x, roots_y, nodes, sides, stack, second, total, roots, low_z, other_z, table):
    table[...] = jnp.zeros_like(table)
    for x in range(2):
        table[COEF + 8 * x : COEF + 8 * x + 8, :16] = coefficient[x]
        table[ZPEN + 8 * x : ZPEN + 8 * x + 8, :17] = z_penalty[x]
    for g in range(3):
        table[XPEN + 8 * g : XPEN + 8 * g + 8, :16] = x_penalty[g]
    for g in range(9):
        table[YPEN + 2 * g : YPEN + 2 * g + 2, :16] = y_penalty[g]
    rooted = jnp.sqrt(jnp.transpose(table[...]))[:24]
    half = lax.broadcasted_iota(jnp.int32, (24, 128), 1) < 64

    def spread(even, odd):
        left = jnp.broadcast_to(rooted[:, even : even + 1], (24, 128))
        right = jnp.broadcast_to(rooted[:, odd : odd + 1], (24, 128))
        return jnp.where(half, left, right)

    for i in range(4):
        for x in range(2):
            roots[0, i, x] = spread(COEF + 8 * x + 2 * i, COEF + 8 * x + 2 * i + 1)
            roots[1, i, x] = spread(XPEN + 16 * x + 2 * i, XPEN + 16 * x + 2 * i + 1)
            roots[2, i, x] = spread(XPEN + 8 + 2 * i, XPEN + 8 + 2 * i + 1)
            roots[3, i, x] = spread(YPEN + 2 * (2 * i + 1) + x, YPEN + 2 * (2 * i + 2) + x)
            roots[4, i, x] = spread(ZPEN + 8 * x + 2 * i, ZPEN + 8 * x + 2 * i + 1)
            roots[5, i, x] = jnp.where(half & (i == 0), jnp.broadcast_to(rooted[:, YPEN + x : YPEN + x + 1], (24, 128)), 0.0)
        roots_x[i] = roots[1, i, 0, :16]
    roots_y[...] = spread(YPEN, YPEN + 1)[:16]

    def relay(i, carry):
        for x in range(2):
            even = lane_tiles(deflation[x, 2 * i])
            odd = lane_tiles(deflation[x, 2 * i + 1])
            for n in range(64):
                a, b, c = n // 16, n // 4 % 4, n % 4
                both = paired(even, odd, NV * n)
                nodes[i, x, pl.ds(n, 16, stride=65), :] = both
                if b % 3 == 0:
                    sides[i, x, b // 3, pl.ds(4 * a + c, 16, stride=17), :] = both
        return carry

    lax.fori_loop(0, 4, relay, 0)
    total[...] = jnp.zeros_like(total)
    node = lax.broadcasted_iota(jnp.int32, (64, 128), 0)

    def edge(position):
        return jnp.where((position == 0) | (position == 3), LINE_WEIGHTS[0], LINE_WEIGHTS[1])

    weight = jnp.sqrt(edge(node // 16) * edge(node // 4 % 4) * edge(node % 4))
    first_half = lax.broadcasted_iota(jnp.int32, (16, 128), 1) < 64

    def fill(step, stack):
        s, i = step // 4, step % 4
        low = jnp.bfloat16

        def root(kind, x, z, rows):
            return jnp.broadcast_to(roots[kind, i, x, pl.ds(z, 1), :], (rows, 128))

        inner = []
        for zz in range(4):
            z = 4 * s + zz
            at = pl.ds(65 * z, 64)
            block = [nodes[i, x, at, :] for x in range(2)]
            z_rows = jnp.concatenate(block, axis=1).astype(low)
            product = jnp.dot(gradients[...], z_rows, preferred_element_type=jnp.float32)
            factor_z = jnp.concatenate([weight * root(0, x, z, 64) for x in range(2)], axis=1)
            for d in range(3):
                stack[192 * zz + 64 * d : 192 * zz + 64 * d + 64, :] = (product[64 * d : 64 * d + 64] * factor_z).astype(low)
            near = (block[0][:16] * root(1, 0, z, 16)).astype(low)
            far = (block[1][48:] * root(1, 1, z, 16)).astype(low)
            stack[768 + 16 * zz : 784 + 16 * zz, :] = jnp.concatenate([near, far], axis=1)
            here = pl.ds(17 * z, 16)
            there = pl.ds(pl.multiple_of(16 * z, 16), 16)
            own_x[i, there, :] = near
            inner.append((root(2, 0, z, 16) * (block[0][48:] - block[1][:16])).astype(low))
            lows, jumps = [], []
            after = jnp.minimum(i + 1, 3)
            for x in range(2):
                lower = sides[i, x, 0, here, :]
                swapped = pltpu.roll(lower, 64, 1)
                later = jnp.where(i < 3, pltpu.roll(sides[after, x, 0, here, :], 64, 1), 0.0)
                jumps.append((root(3, x, z, 16) * (sides[i, x, 1, here, :] - jnp.where(first_half, swapped, later))).astype(low))
                lows.append((root(5, x, z, 16) * lower).astype(low))
            stack[864 + 16 * zz : 880 + 16 * zz, :] = jnp.concatenate(jumps, axis=1)
            stack[928 + 16 * zz : 944 + 16 * zz, :] = jnp.concatenate(lows, axis=1)
            ups, firsts, befores = [], [], []
            for x in range(2):
                upper = nodes[i, x, pl.ds(65 * z + 3, 16, stride=4), :]
                if zz < 3:
                    upper = upper - nodes[i, x, pl.ds(65 * z + 65, 16, stride=4), :]
                ups.append((root(4, x, z + 1, 16) * upper).astype(low))
                if zz == 0:
                    firsts.append((root(4, x, z, 16) * nodes[i, x, pl.ds(65 * z, 16, stride=4), :]).astype(low))
                    before = nodes[i, x, pl.ds(65 * jnp.maximum(z - 1, 0) + 3, 16, stride=4), :]
                    befores.append(jnp.where(s > 0, root(4, x, z, 16) * before, 0.0).astype(low))
            stack[992 + 16 * zz : 1008 + 16 * zz, :] = jnp.concatenate(ups, axis=1)
            if zz == 0:
                stack[1056:1072, :] = jnp.concatenate(firsts, axis=1)
                row = pl.ds(pl.multiple_of(16 * i, 16), 16)
                low_z[s, row, :] = jnp.concatenate(firsts, axis=1)
                other_z[s, row, :] = jnp.concatenate(befores, axis=1)
        stack[832:848, :] = jnp.concatenate(inner[:2], axis=1)
        stack[848:864, :] = jnp.concatenate(inner[2:], axis=1)

    def add(step, stack):
        total[step // 4] += gram(stack[...], stack[...])

    second[...] = jnp.zeros_like(second)

    def pair(step, carry):
        add(jnp.maximum(2 * step - 1, 0), second)
        fill(2 * step, stack)
        add(2 * step, stack)
        fill(2 * step + 1, second)
        return carry

    lax.fori_loop(0, 8, pair, 0)
    add(15, second)

    def folded(square):
        return (
            square[:NV, :128]
            + pltpu.roll(square[64 : 64 + NV, :128], 64, 1)
            + square[128 : 128 + NV, 128:]
            + pltpu.roll(square[192 : 192 + NV, 128:], 64, 1)
        )

    for s in range(4):
        main[s, 0] = folded(total[s])
        below = -folded(gram(low_z[s], other_z[s]))
        main[s, 1] = below
        if s:
            main[s - 1, 2] = jnp.transpose(jnp.concatenate([below, jnp.zeros((80, 128), jnp.float32)], axis=0))[:NV]
    main[3, 2] = jnp.zeros((NV, 128), jnp.float32)
    for z in range(16):
        here = slice(16 * z, 16 * z + 16)
        there = slice(17 * z, 17 * z + 16)
        lower = [sides[0, x, 0, there, :] for x in range(2)]
        near = jnp.where(first_half, lower[0], pltpu.roll(lower[1], 64, 1))
        own_y[here, :] = (near * jnp.broadcast_to(roots_y[z : z + 1, :], (16, 128))).astype(jnp.bfloat16)


def assemble(deflation, gradients, coefficient, x_penalty, y_penalty, z_penalty):
    vmem = pl.BlockSpec(memory_space=pltpu.VMEM)
    f32, low = jnp.float32, jnp.bfloat16
    return pl.pallas_call(
        assemble_kernel,
        out_shape=(
            jax.ShapeDtypeStruct((4, 3, NV, 128), f32),
            jax.ShapeDtypeStruct((4, 256, 128), low),
            jax.ShapeDtypeStruct((256, 128), low),
            jax.ShapeDtypeStruct((4, 16, 128), f32),
            jax.ShapeDtypeStruct((16, 128), f32),
        ),
        in_specs=[vmem] * 6,
        out_specs=(vmem,) * 5,
        scratch_shapes=[
            pltpu.VMEM((4, 2, 1040, 128), f32),
            pltpu.VMEM((4, 2, 2, 272, 128), f32),
            pltpu.VMEM((1072, 256), low),
            pltpu.VMEM((1072, 256), low),
            pltpu.VMEM((4, 256, 256), f32),
            pltpu.VMEM((6, 4, 2, 24, 128), f32),
            pltpu.VMEM((4, 64, 256), low),
            pltpu.VMEM((4, 64, 256), low),
            pltpu.VMEM((128, 128), f32),
        ],
        cost_estimate=pl.CostEstimate(flops=2_000_000_000, bytes_accessed=3_000_000, transcendentals=0),
        name="assemble",
    )(deflation, gradients, coefficient, x_penalty, y_penalty, z_penalty)


def device_index():
    return (lax.axis_index("row") * N_COL + lax.axis_index("col")).astype(jnp.int32)


def flipped(block):
    return jnp.transpose(jnp.concatenate([block, jnp.zeros((80, 128), jnp.float32)], axis=0))[:NV]


def lateral_kernel(order, ranks, below_x, below_y, main, own_x, own_y, roots_x, roots_y, blocks, share, side, plan, halo_x, halo_y):
    device = device_index()
    size = N_ROW * N_COL
    rank_all = ranks[...]
    holder = (lax.broadcasted_iota(jnp.int32, (8, 128), 0) * 128 + lax.broadcasted_iota(jnp.int32, (8, 128), 1)) // SUB_DEV
    first = jnp.sum(jnp.where(rank_all == 0, holder.astype(jnp.float32), 0.0)).astype(jnp.int32)
    distance = (((holder - first + size // 2) & (size - 1)) - size // 2).astype(jnp.float32)
    least = jnp.min(jnp.where(rank_all < PB, distance, float(size))).astype(jnp.int32)
    most = jnp.max(jnp.where(rank_all < PB, distance, float(-size))).astype(jnp.int32)
    base = (first + least) & (size - 1)
    offset = ((base - device + size // 2) & (size - 1)) - size // 2
    near = (most - least) <= 2
    from_below = ((offset + N_COL + 2) & (size - 1)) <= 2
    from_above = ((offset - N_COL + 2) & (size - 1)) <= 2
    beside = (offset >= -3) & (offset <= 1)
    plan[0] = device
    plan[1] = jnp.where(near, jnp.where(beside, offset + 3, jnp.where(from_below, 5, jnp.where(from_above, 6, 0))), 7)
    plan[2] = near.astype(jnp.int32)
    plan[3] = jnp.where(offset == 0, 0, jnp.where(offset == -1, 1, 2))
    for slot in range(12):
        plan[4 + slot] = (base * SUB_DEV + slot) & (SUBS - 1)
    low = jnp.bfloat16
    inside = lax.broadcasted_iota(jnp.int32, (NV, 128), 1) < NV

    def relay(i, carry):
        even = lane_tiles(below_x[2 * i])
        odd = lane_tiles(below_x[2 * i + 1])
        for m in range(16):
            halo_x[i, pl.ds(m, 16, stride=17), :] = paired(even, odd, NV * m) * roots_x[i]
        return carry

    lax.fori_loop(0, 4, relay, 0)
    even = lane_tiles(below_y[0])
    odd = lane_tiles(below_y[1])
    for m in range(16):
        n = 16 * (m // 4) + 12 + m % 4
        halo_y[pl.ds(m, 16, stride=17), :] = paired(even, odd, NV * n) * roots_y[...]

    def folded(square):
        return jnp.where(inside, -(square[:NV] + pltpu.roll(square[64 : 64 + NV], 64, 1)), 0.0)

    diags, low_ys, low_zs = [], [], []
    for s in range(SUB_DEV):
        at = slice(64 * s, 64 * s + 64)
        diag = jnp.where(inside, main[s, 0], 0.0)
        low_z = jnp.where(inside, main[s, 1], 0.0)
        mine = jnp.concatenate([own_x[i, at, :] for i in range(4)], axis=0)
        theirs = [halo_x[i, 17 * z : 17 * z + 16, :].astype(low) for i in range(4) for z in range(4 * s, 4 * s + 4)]
        low_x = folded(gram(mine, jnp.concatenate(theirs, axis=0)))
        theirs = [halo_y[17 * z : 17 * z + 16, :].astype(low) for z in range(4 * s, 4 * s + 4)]
        low_y = folded(gram(own_y[at, :], jnp.concatenate(theirs, axis=0)))
        blocks[s, 0] = diag
        blocks[s, 1] = low_x
        blocks[s, 2] = low_y
        blocks[s, 3] = low_z
        blocks[s, 4] = jnp.where(inside, main[s, 2], 0.0)
        here = device * SUB_DEV + s
        rank = order[here]
        turned_y = jnp.where(rank > order[jnp.maximum(here - SUB_DEV, 0)], low_y, flipped(low_y))
        turned_z = jnp.where(rank > order[jnp.maximum(here - 1, 0)], low_z, flipped(low_z))
        diags.append(diag)
        low_ys.append(turned_y)
        low_zs.append(turned_z)
        if s < 2:
            side[s] = low_x
        else:
            side[s - 2] += pltpu.roll(low_x, 64, 1)
    lane = lax.broadcasted_iota(jnp.int32, (NV, 128), 1)
    row = lax.broadcasted_iota(jnp.int32, (NV, 128), 0)

    def both(lower, upper):
        last = jnp.sum(jnp.where(lane == row, upper, 0.0), axis=1, keepdims=True)
        return jnp.where(lane <= row, lower, upper) + jnp.where(lane == NV, jnp.broadcast_to(last, (NV, 128)), 0.0)

    def piece(start, target):
        moved = pltpu.roll(low_zs[3], (target - start) % 128, 1)
        return jnp.where((lane >= target) & (lane < target + 16), moved, 0.0)

    share[0] = both(diags[0], diags[1]) + pltpu.roll(both(diags[2], diags[3]), 64, 1)
    share[1] = low_ys[0] + pltpu.roll(low_ys[2], 64, 1) + piece(0, 48) + piece(16, 112)
    share[2] = low_ys[1] + pltpu.roll(low_ys[3], 64, 1) + piece(32, 48)
    share[3] = low_zs[1] + pltpu.roll(low_zs[2], 64, 1)


def lateral(order, ranks, below_x, below_y, main, own_x, own_y, roots_x, roots_y):
    smem = pl.BlockSpec(memory_space=pltpu.SMEM)
    vmem = pl.BlockSpec(memory_space=pltpu.VMEM)
    f32 = jnp.float32
    return pl.pallas_call(
        lateral_kernel,
        out_shape=(
            jax.ShapeDtypeStruct((SUB_DEV, 5, NV, 128), f32),
            jax.ShapeDtypeStruct((4, NV, 128), f32),
            jax.ShapeDtypeStruct((2, NV, 128), f32),
            jax.ShapeDtypeStruct((16,), jnp.int32),
        ),
        in_specs=[smem] + [vmem] * 8,
        out_specs=(vmem, vmem, vmem, smem),
        scratch_shapes=[
            pltpu.VMEM((4, 272, 128), f32),
            pltpu.VMEM((272, 128), f32),
        ],
        name="lateral",
    )(order, ranks, below_x, below_y, main, own_x, own_y, roots_x, roots_y)


def row_major(read, write):
    lane = lax.broadcasted_iota(jnp.int32, (8, 128), 1)
    for t in range(18):
        value = None
        for v in range(NV):
            shift = NV * v - 128 * t
            if shift <= -NV or shift >= 128:
                continue
            row = read(v)
            row = pltpu.roll(row, shift % 128, 1) if shift % 128 else row
            here = (lane >= shift) & (lane < shift + NV)
            value = jnp.where(here, row, 0.0 if value is None else value)
        write(t, value)


def flatten_kernel(order, blocks, above, out, high_y, turned):
    device = device_index()
    places = (0, 1, 3, 5, 6)
    for s in range(SUB_DEV):
        for kind in range(5):
            group = (SUB_DEV * kind + s) // 8
            turned[group, pl.ds((SUB_DEV * kind + s) % 8, NV, stride=8), :] = blocks[s, kind]
        packed_low = above[1 + s % 2]
        if s >= 2:
            packed_low = pltpu.roll(packed_low, 64, 1)
        packed_low = jnp.where(lax.broadcasted_iota(jnp.int32, (NV, 128), 1) < NV, packed_low, 0.0)
        here = device * SUB_DEV + s
        later = order[jnp.minimum(here + SUB_DEV, SUBS - 1)]
        upper = jnp.where(order[here] > later, packed_low, flipped(packed_low))
        high_y[s] = upper
        turned[2, pl.ds(SUB_DEV + s, NV, stride=8), :] = upper
    for group in range(3):
        low_place = places[2 * group]
        high_place = places[2 * group + 1] if group < 2 else 4

        def write(t, value):
            out[low_place, :, 128 * t : 128 * t + 128] = value[:4]
            out[high_place, :, 128 * t : 128 * t + 128] = value[4:]

        row_major(lambda v: turned[group, 8 * v : 8 * v + 8, :], write)


def flatten(order, blocks, above):
    smem = pl.BlockSpec(memory_space=pltpu.SMEM)
    vmem = pl.BlockSpec(memory_space=pltpu.VMEM)
    return pl.pallas_call(
        flatten_kernel,
        out_shape=(
            jax.ShapeDtypeStruct((7, SUB_DEV, NV * NV), jnp.float32),
            jax.ShapeDtypeStruct((SUB_DEV, NV, 128), jnp.float32),
        ),
        in_specs=[smem] + [vmem] * 2,
        out_specs=(vmem, vmem),
        scratch_shapes=[pltpu.VMEM((3, NV * 8, 128), jnp.float32)],
        cost_estimate=pl.CostEstimate(flops=1_000_000, bytes_accessed=2_000_000, transcendentals=0),
        name="flatten",
    )(order, blocks, above)


def eliminate(work, unit):
    groups = [work[8 * v : 8 * v + 8] for v in range(6)]
    sub = lax.broadcasted_iota(jnp.int32, (8, 128), 0)

    def row_of(value, k):
        return jnp.broadcast_to(value[k : k + 1, :], (8, 128))

    def column_of(value, k):
        return jnp.broadcast_to(value[:, k : k + 1], (8, 128))

    for g in range(6):
        head = groups[g]
        splat = [column_of(head, 64 + 8 * g + k) * unit for k in range(8)]
        below = [[column_of(groups[v], 64 + 8 * g + k) for k in range(8)] for v in range(g + 1, 6)]
        done = jnp.zeros((8, 128), jnp.float32)
        for k in range(0, 8, 2):
            x, y = splat[k], splat[k + 1]
            a, b, c = row_of(x, k), row_of(y, k), row_of(y, k + 1)
            inverse = 1.0 / (a * c - b * b)
            ratio = b / a
            top, low = row_of(head, k), row_of(head, k + 1)
            done = jnp.where(sub == k, top * lax.rsqrt(a), done)
            done = jnp.where(sub == k + 1, (low - ratio * top) * lax.rsqrt(c - ratio * b), done)

            def reduced(value, upper, lower):
                one = (c * upper - b * lower) * inverse
                two = (a * lower - b * upper) * inverse
                return jnp.where(sub == k, one, jnp.where(sub == k + 1, two, value - x * one - y * two))

            for m in range(k + 2, 8):
                splat[m] = reduced(splat[m], row_of(splat[m], k), row_of(splat[m], k + 1))
            head = reduced(head, top, low)
        rows = [row_of(head, k) for k in range(8)]
        for v in range(g + 1, 6):
            terms = [s * r for s, r in zip(below[v - g - 1], rows)]
            while len(terms) > 1:
                terms = [p + q for p, q in zip(terms[::2], terms[1::2])]
            groups[v] = groups[v] - terms[0]
        groups[g] = done
    return jnp.concatenate(groups, axis=0)


def halves(values):
    high = values.astype(jnp.bfloat16)
    low = (values - high.astype(jnp.float32)).astype(jnp.bfloat16)
    return high, low


def across(left, right):
    return lax.dot_general(left, right, (((1,), (1,)), ((), ())), preferred_element_type=jnp.float32)


ROWS = SUB_DEV * NV
BAND = 4


def factor_kernel(order, meta, own, right1, right2, right3, left1, left2, left3, below, above, rescue, blocks, high_y, flat_in, out, flat, grid, got, dense, lhs, rhs, binv, side, high_x, turned, slab, sems, side_sems):
    device = meta[0]
    lane = lax.broadcasted_iota(jnp.int32, (NV, 128), 1)

    def place(value, half, row, column, wanted):
        parity = column % 2
        moved = pltpu.roll(value, 64 * ((parity + half) % 2), 1)
        inside = (lane >= 64 * parity) & (lane < 64 * parity + NV)
        tile = jnp.where(wanted, column // 2, 7)
        at = pl.ds(pl.multiple_of(jnp.where(wanted, row, 0), 16), NV)
        pltpu.store(grid.at[tile, at, :], moved, mask=inside)

    def ordered(subdomain):
        return order[jnp.clip(subdomain, 0, SUBS - 1)]

    def neighbours(subdomain):
        column = (subdomain // SUB_DEV) % N_COL
        local = subdomain % SUB_DEV
        stride = N_COL * SUB_DEV
        return (
            (subdomain, subdomain >= 0),
            (subdomain - stride, subdomain >= stride),
            (subdomain + stride, (subdomain >= 0) & (subdomain < SUBS - stride)),
            (subdomain - SUB_DEV, (subdomain >= 0) & (column > 0)),
            (subdomain + SUB_DEV, (subdomain >= 0) & (column < N_COL - 1)),
            (subdomain - 1, (subdomain >= 0) & (local > 0)),
            (subdomain + 1, (subdomain >= 0) & (local < SUB_DEV - 1)),
        )

    relevant = jnp.int32(0)
    for l in range(SUB_DEV):
        for near, there in neighbours(device * SUB_DEV + l):
            relevant += (there & (ordered(near) < PB)).astype(jnp.int32)

    side_copy = pltpu.make_async_copy(above.at[pl.ds(12, 2)], side, side_sems.at[0])
    side_copy.start()

    @pl.when(relevant > 0)
    def _():
        near_sources = [right3, right2, right1, own, left1, left2, left3]
        for case in range(5):

            @pl.when(meta[1] == case)
            def _():
                for i in range(3):
                    pltpu.make_async_copy(near_sources[case + i], dense.at[i], sems.at[i]).start()

        for case, source in ((5, below), (6, above)):

            @pl.when(meta[1] == case)
            def _():
                for i in range(3):
                    pltpu.make_async_copy(source.at[pl.ds(4 * i, 4)], dense.at[i], sems.at[i]).start()

        @pl.when(meta[1] == 7)
        def _():
            for i in range(3):
                pltpu.make_async_copy(rescue.at[pl.ds(6 * i, 6)], got.at[i], sems.at[i]).start()

        pltpu.make_async_copy(rescue.at[pl.ds(18, 6)], got.at[3], sems.at[3]).start()

    side_copy.wait()
    for s in range(SUB_DEV):
        packed_low = side[s % 2]
        if s >= 2:
            packed_low = pltpu.roll(packed_low, 64, 1)
        upper = flipped(jnp.where(lane < NV, packed_low, 0.0))
        high_x[s] = upper
        turned[pl.ds(s, NV, stride=8), :] = upper

    def write(t, value):
        slab[:, 128 * t : 128 * t + 128] = value[:4]

    row_major(lambda v: turned[8 * v : 8 * v + 8, :], write)
    flat_copy = pltpu.make_async_copy(slab, flat.at[2], side_sems.at[1])
    flat_copy.start()

    @pl.when(relevant == 0)
    def _():
        out[...] = jnp.zeros_like(out)

    @pl.when(relevant > 0)
    def _():
        grid[:6, : ROWS + PB * NV + BAND * NV, :] = jnp.zeros((6, ROWS + PB * NV + BAND * NV, 128), jnp.float32)
        rhs[...] = jnp.zeros_like(rhs)
        lhs[...] = jnp.zeros_like(lhs)
        for l in range(SUB_DEV):
            for kind, (near, there) in enumerate(neighbours(device * SUB_DEV + l)):
                column = ordered(near)
                value = (blocks.at[l, 0], blocks.at[l, 1], high_x.at[l], blocks.at[l, 2], high_y.at[l], blocks.at[l, 3], blocks.at[l, 4])[kind][...]
                place(value, 0, NV * l, column, there & (column < PB))
        pltpu.make_async_copy(rescue.at[pl.ds(18, 6)], got.at[3], sems.at[3]).wait()

        @pl.when(meta[1] == 7)
        def _():
            for i in range(3):
                pltpu.make_async_copy(rescue.at[pl.ds(6 * i, 6)], got.at[i], sems.at[i]).wait()

        @pl.when(meta[1] < 7)
        def _():
            row = lax.broadcasted_iota(jnp.int32, (NV, 128), 0)
            left = lane < 64
            for i in range(3):
                pltpu.make_async_copy(own, dense.at[i], sems.at[i]).wait()
                pairs = dense[i, 0]
                whole = []
                for half in range(2):
                    slot = pltpu.roll(pairs, 64, 1) if half else pairs
                    last = jnp.broadcast_to(slot[:, NV : NV + 1], (NV, 128))
                    turned_slot = flipped(jnp.where(lane < NV, slot, 0.0))
                    whole.append(jnp.where(lane <= row, slot, turned_slot))
                    whole.append(jnp.where(lane == row, last, jnp.where(lane < row, turned_slot, slot)))
                got[i, 0] = jnp.where(left, whole[0], pltpu.roll(whole[2], 64, 1))
                got[i, 3] = jnp.where(left, whole[1], pltpu.roll(whole[3], 64, 1))
                got[i, 1] = dense[i, 1]
                got[i, 4] = dense[i, 2]
                z_pair = dense[i, 3]
                z_last = jnp.where(
                    lane < 80,
                    pltpu.roll(dense[i, 1], 16, 1),
                    jnp.where(lane < 96, pltpu.roll(dense[i, 1], 96, 1), pltpu.roll(dense[i, 2], 48, 1)),
                )
                got[i, 2] = z_pair
                got[i, 5] = jnp.where(left, z_pair, z_last)
        reach = jnp.int32(0)
        for slot in range(12):
            i, l = slot // SUB_DEV, slot % SUB_DEV
            s = meta[4 + slot]
            p = ordered(s)
            near = neighbours(s)
            for kind, (t, there) in enumerate((near[0], near[3], near[5], near[1])):
                q = ordered(t)
                wanted = there & (p < PB) & (q < PB)
                reach = jnp.maximum(reach, jnp.where(wanted, jnp.abs(p - q), 0))
                if kind < 3:
                    place(got[i, (l % 2) * 3 + kind], l // 2, ROWS + NV * jnp.maximum(p, q), jnp.minimum(p, q), wanted)

        @pl.when(meta[1] == 7)
        def _():
            for slot in range(12):
                s = meta[4 + slot]
                p = ordered(s)
                t, there = neighbours(s)[1]
                q = ordered(t)
                place(got[3, slot % 6], slot // 6, ROWS + NV * jnp.maximum(p, q), jnp.minimum(p, q), there & (p < PB) & (q < PB))

        rows48 = lax.broadcasted_iota(jnp.int32, (NV, 128), 0)

        unit = jnp.full((8, 128), jnp.where(device >= 0, 1.0, 0.0), jnp.float32)

        gap = jnp.zeros((16, 128), jnp.bfloat16)

        def diagonal(k):
            at = pl.ds(pl.multiple_of(ROWS + k * NV, 16), NV)
            return pltpu.roll(grid[k // 2, at, :], 64 * (1 - k % 2), 1)

        def invert(k, diag):
            work = jnp.where(lane < 64, (lane == rows48).astype(jnp.float32), jnp.where(lane < 64 + NV, diag, 0.0))
            inverse = jnp.where(lane < NV, eliminate(work, unit), 0.0)
            high, low = halves(pltpu.roll(inverse, 64 * (k % 2), 1))
            binv[0] = jnp.concatenate([high, gap, high, gap], axis=0)
            binv[1] = jnp.concatenate([low, gap, low, gap], axis=0)
            high, low = halves(inverse)
            return jnp.concatenate([high, gap, high, gap], axis=0), jnp.concatenate([low, gap, low, gap], axis=0)

        def solve(values, high, low):
            c_high, c_low = halves(values)
            return across(jnp.concatenate([c_high, c_low], axis=1), jnp.concatenate([high, high], axis=1)) + across(c_high, low)

        def mix(high, low):
            left_half = lax.broadcasted_iota(jnp.int32, high.shape, 1) < 64
            return jnp.where(left_half, high.astype(jnp.float32), low.astype(jnp.float32)).astype(jnp.bfloat16)

        def urgent(k, high, low):
            at = pl.ds(pl.multiple_of(ROWS + (k + 1) * NV, 16), NV)
            ahead = pltpu.roll(grid[k // 2, at, :], 64 * (k % 2), 1)
            following = diagonal(k + 1)
            s_high, s_low = halves(solve(ahead, high, low))
            mixed = mix(s_high, s_low)
            other = jnp.concatenate([mixed, gap, mixed, gap], axis=0)
            change = across(jnp.concatenate([s_high, s_low], axis=1), jnp.concatenate([other, other], axis=1))
            mine = lane // 64 == (k + 1) % 2
            grid[(k + 1) // 2, at, :] -= jnp.where(mine, change, 0.0)
            return following - change

        def finish(band, k, live):
            tile = k // 2
            depth = ROWS + band * NV
            window = pl.ds(pl.multiple_of(ROWS + k * NV, 16), NV + band * NV)
            later = pl.ds(pl.multiple_of(ROWS + (k + 1) * NV, 16), band * NV)
            at = pl.ds(pl.multiple_of(ROWS + k * NV, 16), NV)
            column = jnp.concatenate([grid[tile, :ROWS, :], grid[tile, window, :]], axis=0)
            solved = solve(column, binv[0], binv[1])
            corner = jnp.where((lane % 64) <= rows48, solved[ROWS : ROWS + NV], 0.0)
            parity = jnp.where(live, k % 2, 2)
            rest = jnp.concatenate([solved[:ROWS], solved[ROWS + NV :]], axis=0)
            chosen = lax.broadcasted_iota(jnp.int32, (depth, 128), 1) // 64 == parity
            kept = jnp.where(chosen, rest, jnp.concatenate([column[:ROWS], column[ROWS + NV :]], axis=0))
            grid[tile, :ROWS, :] = kept[:ROWS]
            grid[tile, later, :] = kept[ROWS:]
            grid[tile, at, :] = jnp.where(lane // 64 == parity, corner, column[ROWS : ROWS + NV])
            s_high, s_low = halves(rest)
            lhs[:depth, :128] = s_high
            lhs[:depth, 128:] = s_low
            mixed = mix(s_high[ROWS:], s_low[ROWS:])
            rhs[pl.ds(pl.multiple_of(64 * k, 64), 64), :] = jnp.zeros((64, 128), jnp.bfloat16)
            for w in range(band):
                rhs[pl.ds(pl.multiple_of(64 * (k + 1 + w), 64), NV), :] = mixed[NV * w : NV * w + NV]

        def trail(band, k, t, skip):
            depth = ROWS + band * NV
            later = pl.ds(pl.multiple_of(ROWS + (k + 1 + skip) * NV, 16), (band - skip) * NV)
            other = rhs[pl.ds(pl.multiple_of(128 * t, 128), 128), :]
            other = jnp.concatenate([other, other], axis=1)
            grid[t, :ROWS, :] -= across(lhs[:ROWS, :], other)
            grid[t, later, :] -= across(lhs[ROWS + skip * NV : depth, :], other)

        @pl.when(reach <= BAND)
        def _():
            binv[...] = jnp.zeros_like(binv)

            def body(k, carry):
                diag = carry
                last = jnp.maximum(k - 1, 0)
                finish(BAND, last, k > 0)
                for j in range(3):
                    trail(BAND, last, k // 2 + j, 1 if j == 0 else 0)
                high, low = invert(k, diag)
                return urgent(k, high, low)

            lax.fori_loop(0, PB, body, diagonal(0))
            finish(BAND, PB - 1, True)

        @pl.when(reach > BAND)
        def _():
            start = ROWS + PB * NV + BAND * NV
            grid[:6, start:, :] = jnp.zeros((6, grid.shape[1] - start, 128), jnp.float32)

            def body(k, carry):
                invert(k, diagonal(k))
                finish(PB - 1, k, True)

                def inner(t, c):
                    trail(PB - 1, k, t, 0)
                    return c

                lax.fori_loop((k + 1) // 2, 6, inner, 0)
                return carry

            lax.fori_loop(0, PB, body, 0)

        for l in range(SUB_DEV):
            p = ordered(device * SUB_DEV + l)
            inside = p < PB
            start = jnp.where(inside, ROWS + NV * p, NV * l)
            at = pl.ds(pl.multiple_of(start, 16), NV)
            pieces = []
            for j in range(PB):
                piece = grid[j // 2, at, :][:, 64 * (j % 2) : 64 * (j % 2) + NV]
                pieces.append(jnp.where(inside & (j > p), 0.0, piece))
            out[l] = jnp.concatenate(pieces, axis=1)

    flat_copy.wait()


def factor(order, meta, shares, below, above, rescue, blocks, high_y, flat):
    smem = pl.BlockSpec(memory_space=pltpu.SMEM)
    hbm = pl.BlockSpec(memory_space=pl.ANY)
    vmem = pl.BlockSpec(memory_space=pltpu.VMEM)
    return pl.pallas_call(
        factor_kernel,
        out_shape=(
            jax.ShapeDtypeStruct((SUB_DEV, NV, PB * NV), jnp.float32),
            jax.ShapeDtypeStruct(flat.shape, jnp.float32),
        ),
        in_specs=[smem] * 2 + [hbm] * 10 + [vmem] * 2 + [hbm],
        out_specs=(vmem, hbm),
        input_output_aliases={14: 1},
        scratch_shapes=[
            pltpu.VMEM((8, ROWS + PB * NV + PB * NV, 128), jnp.float32),
            pltpu.VMEM((4, 6, NV, 128), jnp.float32),
            pltpu.VMEM((3, 4, NV, 128), jnp.float32),
            pltpu.VMEM((ROWS + (PB - 1) * NV, 256), jnp.bfloat16),
            pltpu.VMEM(((2 * PB + 2) * 64, 128), jnp.bfloat16),
            pltpu.VMEM((2, 128, 128), jnp.bfloat16),
            pltpu.VMEM((2, NV, 128), jnp.float32),
            pltpu.VMEM((SUB_DEV, NV, 128), jnp.float32),
            pltpu.VMEM((NV * 8, 128), jnp.float32),
            pltpu.VMEM((SUB_DEV, NV * NV), jnp.float32),
            pltpu.SemaphoreType.DMA((4,)),
            pltpu.SemaphoreType.DMA((2,)),
        ],
        name="factor",
    )(order, meta, *shares, below, above, rescue, blocks, high_y, flat)


def shifted(value, amount):
    size = N_ROW * N_COL
    return lax.ppermute(value, ("row", "col"), [(i, (i + amount) % size) for i in range(size)])


def packed(blocks):
    wide = jnp.pad(blocks, ((0, 0), (0, 0), (0, 64 - NV)))
    return jnp.concatenate([wide[:6], wide[6:]], axis=2)


def everywhere(value):
    size = N_ROW * N_COL
    step = 1
    while step < size:
        value = value + lax.ppermute(value, ("row", "col"), [(i, i ^ step) for i in range(size)])
        step *= 2
    return value


def choose_kernel(spot, right2, right1, share, left1, left2, side, out):
    out[12:14] = side[...]
    for case, sources in enumerate(((share, left1, left2), (right1, share, left1), (right2, right1, share))):

        @pl.when(spot[3] == case)
        def _():
            for i, source in enumerate(sources):
                out[4 * i : 4 * i + 4] = source[...]


def choose(spot, right2, right1, share, left1, left2, side):
    vmem = pl.BlockSpec(memory_space=pltpu.VMEM)
    return pl.pallas_call(
        choose_kernel,
        out_shape=jax.ShapeDtypeStruct((14, NV, 128), jnp.float32),
        in_specs=[pl.BlockSpec(memory_space=pltpu.SMEM)] + [vmem] * 6,
        out_specs=vmem,
        name="choose",
    )(spot, right2, right1, share, left1, left2, side)


def exchange(device, order, blocks, share, side, plan):
    subdomain = jnp.arange(SUBS, dtype=jnp.int32)
    my_order = lax.dynamic_slice(order, (device * SUB_DEV,), (SUB_DEV,))

    right1 = shifted(share, 1)
    left1 = shifted(share, -1)
    right2 = shifted(share, 2)
    left2 = shifted(share, -2)
    payload = choose(plan, right2, right1, share, left1, left2, side)
    below = shifted(payload, N_COL)
    above = shifted(payload, -N_COL)
    flat, high_y = flatten(order, blocks, left1)
    right3 = shifted(right2, 1)
    left3 = shifted(left2, -1)
    def local_path(_):
        return (jnp.zeros((24, NV, 128), jnp.float32), plan)

    def global_path(_):
        slots = jnp.arange(12, dtype=jnp.int32)
        hit = (order[None, :] == slots[:, None]) & (slots[:, None] < PB)
        listed = jnp.where(slots < PB, jnp.sum(jnp.where(hit, subdomain[None, :], 0), axis=1), -1)
        mask = ((my_order[None, :] == slots[:, None]) & (slots[:, None] < PB)).astype(jnp.float32)
        def oriented(block, offset):
            other = lax.dynamic_slice(jnp.concatenate([order[:128], order]), (128 + device * SUB_DEV - offset,), (SUB_DEV,))
            return jnp.where((my_order > other)[:, None, None], block, jnp.swapaxes(block, 1, 2))

        kinds = jnp.stack(
            [
                blocks[:, 0, :, :NV],
                oriented(blocks[:, 2, :, :NV], SUB_DEV),
                oriented(blocks[:, 3, :, :NV], 1),
                oriented(blocks[:, 1, :, :NV], N_COL * SUB_DEV),
            ],
            axis=1,
        )
        placed = jnp.einsum("ps,skvw->pkvw", mask, kinds, precision=lax.Precision.HIGHEST)
        whole = everywhere(
            jnp.stack([packed(placed[4 * i : 4 * i + 4, :3].reshape(12, NV, NV)) for i in range(3)] + [packed(placed[:, 3])])
        )
        return (whole.reshape(24, NV, 128), jnp.concatenate([plan[:4], listed]).astype(jnp.int32))

    rescue, meta = lax.cond(plan[2] > 0, local_path, global_path, None)
    shares = (share, right1, right2, right3, left1, left2, left3)
    panel, flat = factor(order, meta, shares, below, above, rescue, blocks, high_y, flat)
    return (jnp.transpose(flat, (1, 0, 2)), panel)


def edges_kernel(deflation, along_x, along_y, sems):
    x_copy = pltpu.make_async_copy(deflation.at[1, :, :, pl.ds(48 * NV, 16 * NV)], along_x, sems.at[0])
    y_copies = [pltpu.make_async_copy(deflation.at[x, 7], along_y.at[x], sems.at[1 + x]) for x in range(2)]
    x_copy.start()
    for copy in y_copies:
        copy.start()
    x_copy.wait()
    for copy in y_copies:
        copy.wait()


def edges(deflation):
    vmem = pl.BlockSpec(memory_space=pltpu.VMEM)
    return pl.pallas_call(
        edges_kernel,
        out_shape=(
            jax.ShapeDtypeStruct((8, 16, 16 * NV), jnp.bfloat16),
            jax.ShapeDtypeStruct((2, 16, 64 * NV), jnp.bfloat16),
        ),
        in_specs=[pl.BlockSpec(memory_space=pl.ANY)],
        out_specs=(vmem, vmem),
        scratch_shapes=[pltpu.SemaphoreType.DMA((3,))],
        name="edges",
    )(deflation)


def from_next(value, axis, amount):
    size = lax.axis_size(axis)
    pairs = [(i, i + amount) for i in range(size) if 0 <= i + amount < size]
    return lax.ppermute(value, axis, pairs)


def shards(deflation, coefficient, gradients, x_penalty, y_penalty, z_penalty, coarse_order):
    device = device_index()
    along_x, along_y = edges(deflation)
    below_x = from_next(along_x, "row", 1)
    below_y = from_next(along_y, "col", 1)
    main, own_x, own_y, roots_x, roots_y = assemble(
        deflation, gradients.reshape(192, 64), coefficient, x_penalty, jnp.transpose(y_penalty, (1, 0, 2)), z_penalty
    )
    blocks, share, side, plan = lateral(coarse_order, coarse_order.reshape(8, 128), below_x, below_y, main, own_x, own_y, roots_x, roots_y)
    return exchange(device, coarse_order, blocks, share, side, plan)


def solution(mesh):
    in_specs = (
        P("row", "col", None, None),
        P("row", "col", None),
        P(),
        P("row", "col", None),
        P("row", "col", None),
        P("row", "col", None),
        P(),
    )
    out_specs = (P(("row", "col"), None, None), P(("row", "col"), None, None))
    return jax.shard_map(shards, mesh=mesh, in_specs=in_specs, out_specs=out_specs, check_vma=False)
```

profile of v0, /device:TPU:3, one launch (start us, length us, event | category | flops | bytes accessed | tf_op | source)
XLA Modules:
  0.0 75.8 jit_solution(15190166423640412645)
XLA Ops:
  0.6 1.8 %edges.1 = (bf16[8,16,768]{2,1,0:T(8,128)(2,1)}, bf16[2,16,3072]{2,1,0:T(8,128)(2,1)}) custom-call(bf16[2,8,16,3072]{3,2,1,0:T(8,128)(2,1)} %deflation.3), custom_call_target="tpu_custom_call" | custom-call | tf_op jit(solution)/shard_map/edges/pallas_call | solution.py:841
  2.4 3.7 %collective-permute-start.8 = (bf16[8,16,768]{2,1,0:T(8,128)(2,1)}, bf16[8,16,768]{2,1,0:T(8,128)(2,1)S(1)}, u32[]{:S(2)}, u32[]{:S(2)}) collective-permute-start(bf16[8,16,768]{2,1,0:T(8,128)(2,1)} %get-tuple-element.38), channel_id=1, source_target_pairs={{0,32},{32,64},{64,96},{96,128},{128,160},{160,192},{192,224},{1,3... | collective-permute-start | bytes 589832 | tf_op jit(solution)/shard_map/ppermute | solution.py:857
  6.1 3.6 %collective-permute-start.9 = (bf16[2,16,3072]{2,1,0:T(8,128)(2,1)}, bf16[2,16,3072]{2,1,0:T(8,128)(2,1)S(1)}, u32[]{:S(2)}, u32[]{:S(2)}) collective-permute-start(bf16[2,16,3072]{2,1,0:T(8,128)(2,1)} %get-tuple-element.39), channel_id=1, source_target_pairs={{0,1},{1,2},{2,3},{3,4},{4,5},{5,6},{6,7},{7,8},{8,9},{9,10},{10,1... | collective-permute-start | bytes 589832 | tf_op jit(solution)/shard_map/ppermute | solution.py:857
  9.7 0.0 copy-start.6
  9.7 11.6 %assemble.1 = (f32[4,3,48,128]{3,2,1,0:T(8,128)}, bf16[4,256,128]{2,1,0:T(8,128)(2,1)}, bf16[256,128]{1,0:T(8,128)(2,1)}, f32[4,16,128]{2,1,0:T(8,128)}, f32[16,128]{1,0:T(8,128)}) custom-call(bf16[2,8,16,3072]{3,2,1,0:T(8,128)(2,1)} %deflation.3, bf16[192,64]{1,0:T(8,128)(2,1)} %bitcast.61, f32[2,8,16]{2,1,0:T(8,128)} %coefficient.1, ...), custom_call_target="tpu_custom_call" | custom-call | flops 2000000000 | bytes 3000000 | tf_op jit(solution)/shard_map/assemble/pallas_call | solution.py:189
  21.3 0.0 collective-permute-done.8.below_x
  21.3 0.0 copy-start.7
  21.3 0.0 collective-permute-done.9.below_y
  21.3 0.6 copy-done.7
  22.0 0.1 copy-done.8
  22.0 3.4 %lateral.1 = (f32[4,5,48,128]{3,2,1,0:T(8,128)S(1)}, f32[4,48,128]{2,1,0:T(8,128)}, f32[2,48,128]{2,1,0:T(8,128)}, s32[16]{0:T(128)S(1)}) custom-call(s32[1024]{0:T(1024)S(1)} %copy-done.6, s32[8,128]{1,0:T(8,128)S(1)} %bitcast.59, bf16[8,16,768]{2,1,0:T(8,128)(2,1)} %copy-done.7, bf16[2,16,3072]{2,1,0:T(8,128)(2,1)} %copy-done.8, ...), custom_call_target="tpu_custom_call" | custom-call | tf_op jit(solution)/shard_map/lateral/pallas_call | solution.py:312
  25.4 1.7 %collective-permute-start.10 = (f32[4,48,128]{2,1,0:T(8,128)}, f32[4,48,128]{2,1,0:T(8,128)S(1)}, u32[]{:S(2)}, u32[]{:S(2)}) collective-permute-start(f32[4,48,128]{2,1,0:T(8,128)} %get-tuple-element.48.share.own), channel_id=1, source_target_pairs={{0,1},{1,2},{2,3},{3,4},{4,5},{5,6},{6,7},{7,8},{8,9},{9,10},{10,1... | collective-permute-start | bytes 294920 | tf_op jit(solution)/shard_map/ppermute | solution.py:743
  27.1 4.2 %collective-permute-start.11 = (f32[4,48,128]{2,1,0:T(8,128)}, f32[4,48,128]{2,1,0:T(8,128)S(1)}, u32[]{:S(2)}, u32[]{:S(2)}) collective-permute-start(f32[4,48,128]{2,1,0:T(8,128)} %get-tuple-element.48.share.own), channel_id=1, source_target_pairs={{0,2},{1,3},{2,4},{3,5},{4,6},{5,7},{6,8},{7,9},{8,10},{9,11},{10,... | collective-permute-start | bytes 294920 | tf_op jit(solution)/shard_map/ppermute | solution.py:743
  31.3 2.2 %collective-permute-start.13 = (f32[4,48,128]{2,1,0:T(8,128)}, f32[4,48,128]{2,1,0:T(8,128)S(1)}, u32[]{:S(2)}, u32[]{:S(2)}) collective-permute-start(f32[4,48,128]{2,1,0:T(8,128)} %get-tuple-element.48.share.own), channel_id=1, source_target_pairs={{0,255},{1,0},{2,1},{3,2},{4,3},{5,4},{6,5},{7,6},{8,7},{9,8},{10,... | collective-permute-start | bytes 294920 | tf_op jit(solution)/shard_map/ppermute | solution.py:743
  33.6 0.6 collective-permute-start.14
  34.2 0.0 collective-permute-done.10.right1
  34.2 3.6 %collective-permute-done.11.right2 = f32[4,48,128]{2,1,0:T(8,128)S(1)} collective-permute-done((f32[4,48,128]{2,1,0:T(8,128)}, f32[4,48,128]{2,1,0:T(8,128)S(1)}, u32[]{:S(2)}, u32[]{:S(2)}) %collective-permute-start.11) | collective-permute-done | bytes 98336 | tf_op jit(solution)/shard_map/ppermute | solution.py:743
  37.8 0.0 collective-permute-done.13.left1.above
  37.8 3.5 %collective-permute-done.14.left2 = f32[4,48,128]{2,1,0:T(8,128)S(1)} collective-permute-done((f32[4,48,128]{2,1,0:T(8,128)}, f32[4,48,128]{2,1,0:T(8,128)S(1)}, u32[]{:S(2)}, u32[]{:S(2)}) %collective-permute-start.14) | collective-permute-done | bytes 98336 | tf_op jit(solution)/shard_map/ppermute | solution.py:743
  41.3 0.6 copy-done.3
  41.9 1.9 %choose.1 = f32[14,48,128]{2,1,0:T(8,128)} custom-call(s32[16]{0:T(128)S(1)} %get-tuple-element.45.spot, f32[4,48,128]{2,1,0:T(8,128)} %copy-done.2, f32[4,48,128]{2,1,0:T(8,128)} %copy-done.1, f32[4,48,128]{2,1,0:T(8,128)} %get-tuple-element.48.share.own, f32[4,48,128]{2,1,0:T(8,128)} %copy-done, f32[4,48,128]{2,1,0:T(8,128)} %copy-done.3, ...), custom_call_target="tpu_custom_call" | custom-call | tf_op jit(solution)/shard_map/choose/pallas_call | solution.py:772
  43.8 1.2 %collective-permute-start.16 = (f32[14,48,128]{2,1,0:T(8,128)}, f32[14,48,128]{2,1,0:T(8,128)S(1)}, u32[]{:S(2)}, u32[]{:S(2)}) collective-permute-start(f32[14,48,128]{2,1,0:T(8,128)} %choose.1), channel_id=1, source_target_pairs={{0,32},{1,33},{2,34},{3,35},{4,36},{5,37},{6,38},{7,39},{8,40},{9,... | collective-permute-start | bytes 1032200 | tf_op jit(solution)/shard_map/ppermute | solution.py:743
  45.0 0.0 collective-permute-start.17
  45.0 0.0 collective-permute-start.12
  45.0 5.1 %collective-permute-start.15 = (f32[4,48,128]{2,1,0:T(8,128)}, f32[4,48,128]{2,1,0:T(8,128)}, u32[]{:S(2)}, u32[]{:S(2)}) collective-permute-start(f32[4,48,128]{2,1,0:T(8,128)} %copy-done.3), channel_id=1, source_target_pairs={{0,255},{1,0},{2,1},{3,2},{4,3},{5,4},{6,5},{7,6},{8,7},{9,8},{10,... | collective-permute-start | bytes 294920 | tf_op jit(solution)/shard_map/ppermute | solution.py:743
  50.1 0.6 slice.59
  51.3 0.3 conditional.1
  51.6 1.9 %flatten.1 = (f32[7,4,2304]{2,1,0:T(4,128)}, f32[4,48,128]{2,1,0:T(8,128)}) custom-call(s32[1024]{0:T(1024)S(1)} %copy-done.6, f32[4,5,48,128]{3,2,1,0:T(8,128)S(1)} %get-tuple-element.46.blocks, f32[4,48,128]{2,1,0:T(8,128)} %copy-done), custom_call_target="tpu_custom_call" | custom-call | flops 1000000 | bytes 2000000 | tf_op jit(solution)/shard_map/flatten/pallas_call | solution.py:375
  53.6 0.6 copy-done.9
  54.2 0.2 copy-done.4
  54.3 0.1 copy-done.5
  54.5 21.2 %factor.1 = (f32[4,48,528]{2,1,0:T(8,128)}, f32[7,4,2304]{2,1,0:T(4,128)}) custom-call(s32[1024]{0:T(1024)S(1)} %copy-done.6, s32[16]{0:T(128)S(1)} %get-tuple-element.47.meta, f32[4,48,128]{2,1,0:T(8,128)} %get-tuple-element.48.share.own, f32[4,48,128]{2,1,0:T(8,128)} %copy-done.1, f32[4,48,128]{2,1,0:T(8,128)} %copy-done.2, ...), custom_call_target="tpu_custom_call", output_to_operand_aliasing={{1}: (14, {})} | custom-call | tf_op jit(solution)/shard_map/factor/pallas_call | solution.py:714
  (18 shorter events, 0.1 us)
Async XLA Ops:
  2.4 18.8 %collective-permute-start.8 = (bf16[8,16,768]{2,1,0:T(8,128)(2,1)}, bf16[8,16,768]{2,1,0:T(8,128)(2,1)S(1)}, u32[]{:S(2)}, u32[]{:S(2)}) collective-permute-start(bf16[8,16,768]{2,1,0:T(8,128)(2,1)} %get-tuple-element.38), channel_id=1, source_target_pairs={{0,32},{32,64},{64,96},{96,128},{128,160},{160,192},{192,224},{1,3... | collective-permute-start | bytes 589832 | tf_op jit(solution)/shard_map/ppermute | solution.py:857
  6.1 15.2 %collective-permute-start.9 = (bf16[2,16,3072]{2,1,0:T(8,128)(2,1)}, bf16[2,16,3072]{2,1,0:T(8,128)(2,1)S(1)}, u32[]{:S(2)}, u32[]{:S(2)}) collective-permute-start(bf16[2,16,3072]{2,1,0:T(8,128)(2,1)} %get-tuple-element.39), channel_id=1, source_target_pairs={{0,1},{1,2},{2,3},{3,4},{4,5},{5,6},{6,7},{7,8},{8,9},{9,10},{10,1... | collective-permute-start | bytes 589832 | tf_op jit(solution)/shard_map/ppermute | solution.py:857
  9.7 12.3 %copy-start.6 = (s32[1024]{0:T(1024)S(1)}, s32[1024]{0:T(1024)}, u32[]{:S(2)}) copy-start(s32[1024]{0:T(1024)} %order.5) | copy-start | bytes 12292
  21.3 0.7 copy-start.7
  21.3 0.7 copy-start.8
  25.4 8.8 %collective-permute-start.10 = (f32[4,48,128]{2,1,0:T(8,128)}, f32[4,48,128]{2,1,0:T(8,128)S(1)}, u32[]{:S(2)}, u32[]{:S(2)}) collective-permute-start(f32[4,48,128]{2,1,0:T(8,128)} %get-tuple-element.48.share.own), channel_id=1, source_target_pairs={{0,1},{1,2},{2,3},{3,4},{4,5},{5,6},{6,7},{7,8},{8,9},{9,10},{10,1... | collective-permute-start | bytes 294920 | tf_op jit(solution)/shard_map/ppermute | solution.py:743
  27.1 10.6 %collective-permute-start.11 = (f32[4,48,128]{2,1,0:T(8,128)}, f32[4,48,128]{2,1,0:T(8,128)S(1)}, u32[]{:S(2)}, u32[]{:S(2)}) collective-permute-start(f32[4,48,128]{2,1,0:T(8,128)} %get-tuple-element.48.share.own), channel_id=1, source_target_pairs={{0,2},{1,3},{2,4},{3,5},{4,6},{5,7},{6,8},{7,9},{8,10},{9,11},{10,... | collective-permute-start | bytes 294920 | tf_op jit(solution)/shard_map/ppermute | solution.py:743
  31.3 6.4 %collective-permute-start.13 = (f32[4,48,128]{2,1,0:T(8,128)}, f32[4,48,128]{2,1,0:T(8,128)S(1)}, u32[]{:S(2)}, u32[]{:S(2)}) collective-permute-start(f32[4,48,128]{2,1,0:T(8,128)} %get-tuple-element.48.share.own), channel_id=1, source_target_pairs={{0,255},{1,0},{2,1},{3,2},{4,3},{5,4},{6,5},{7,6},{8,7},{9,8},{10,... | collective-permute-start | bytes 294920 | tf_op jit(solution)/shard_map/ppermute | solution.py:743
  33.6 7.7 %collective-permute-start.14 = (f32[4,48,128]{2,1,0:T(8,128)}, f32[4,48,128]{2,1,0:T(8,128)S(1)}, u32[]{:S(2)}, u32[]{:S(2)}) collective-permute-start(f32[4,48,128]{2,1,0:T(8,128)} %get-tuple-element.48.share.own), channel_id=1, source_target_pairs={{0,254},{1,255},{2,0},{3,1},{4,2},{5,3},{6,4},{7,5},{8,6},{9,7},{1... | collective-permute-start | bytes 294920 | tf_op jit(solution)/shard_map/ppermute | solution.py:743
  34.2 7.1 %copy-start.1 = (f32[4,48,128]{2,1,0:T(8,128)}, f32[4,48,128]{2,1,0:T(8,128)S(1)}, u32[]{:S(2)}) copy-start(f32[4,48,128]{2,1,0:T(8,128)S(1)} %collective-permute-done.10.right1) | copy-start | bytes 294916
  37.8 3.5 %copy-start.2 = (f32[4,48,128]{2,1,0:T(8,128)}, f32[4,48,128]{2,1,0:T(8,128)S(1)}, u32[]{:S(2)}) copy-start(f32[4,48,128]{2,1,0:T(8,128)S(1)} %collective-permute-done.11.right2) | copy-start | bytes 294916
  37.8 3.5 %copy-start = (f32[4,48,128]{2,1,0:T(8,128)}, f32[4,48,128]{2,1,0:T(8,128)S(1)}, u32[]{:S(2)}) copy-start(f32[4,48,128]{2,1,0:T(8,128)S(1)} %collective-permute-done.13.left1.above) | copy-start | bytes 294916
  41.3 0.6 copy-start.3
  43.8 9.8 %collective-permute-start.16 = (f32[14,48,128]{2,1,0:T(8,128)}, f32[14,48,128]{2,1,0:T(8,128)S(1)}, u32[]{:S(2)}, u32[]{:S(2)}) collective-permute-start(f32[14,48,128]{2,1,0:T(8,128)} %choose.1), channel_id=1, source_target_pairs={{0,32},{1,33},{2,34},{3,35},{4,36},{5,37},{6,38},{7,39},{8,40},{9,... | collective-permute-start | bytes 1032200 | tf_op jit(solution)/shard_map/ppermute | solution.py:743
  45.0 8.6 %collective-permute-start.17 = (f32[14,48,128]{2,1,0:T(8,128)}, f32[14,48,128]{2,1,0:T(8,128)S(1)}, u32[]{:S(2)}, u32[]{:S(2)}) collective-permute-start(f32[14,48,128]{2,1,0:T(8,128)} %choose.1), channel_id=1, source_target_pairs={{0,224},{1,225},{2,226},{3,227},{4,228},{5,229},{6,230},{7,231},{8... | collective-permute-start | bytes 1032200 | tf_op jit(solution)/shard_map/ppermute | solution.py:743
  45.0 8.5 %collective-permute-start.12 = (f32[4,48,128]{2,1,0:T(8,128)}, f32[4,48,128]{2,1,0:T(8,128)S(1)}, u32[]{:S(2)}, u32[]{:S(2)}) collective-permute-start(f32[4,48,128]{2,1,0:T(8,128)} %copy-done.2), channel_id=1, source_target_pairs={{0,1},{1,2},{2,3},{3,4},{4,5},{5,6},{6,7},{7,8},{8,9},{9,10},{10,1... | collective-permute-start | bytes 294920 | tf_op jit(solution)/shard_map/ppermute | solution.py:743
  45.0 8.6 %collective-permute-start.15 = (f32[4,48,128]{2,1,0:T(8,128)}, f32[4,48,128]{2,1,0:T(8,128)}, u32[]{:S(2)}, u32[]{:S(2)}) collective-permute-start(f32[4,48,128]{2,1,0:T(8,128)} %copy-done.3), channel_id=1, source_target_pairs={{0,255},{1,0},{2,1},{3,2},{4,3},{5,4},{6,5},{7,6},{8,7},{9,8},{10,... | collective-permute-start | bytes 294920 | tf_op jit(solution)/shard_map/ppermute | solution.py:743
  53.6 0.6 copy-start.9
  53.6 0.8 %copy-start.4 = (f32[14,48,128]{2,1,0:T(8,128)}, f32[14,48,128]{2,1,0:T(8,128)S(1)}, u32[]{:S(2)}) copy-start(f32[14,48,128]{2,1,0:T(8,128)S(1)} %collective-permute-done.16.below) | copy-start | bytes 1032196
  53.6 0.9 %copy-start.5 = (f32[14,48,128]{2,1,0:T(8,128)}, f32[14,48,128]{2,1,0:T(8,128)S(1)}, u32[]{:S(2)}) copy-start(f32[14,48,128]{2,1,0:T(8,128)S(1)} %collective-permute-done.17.above) | copy-start | bytes 1032196
where the time goes:
time: 75.1 us; the launch traced here: 75.8 us
  Pallas kernels  41.7 us (56%)
  starting transfers between devices  22.3 us (30%)
  waiting for transfers between devices  7.09 us (9%)
  local copies, waits for them, and re-layouts  2.84 us (4%)
  between operations  1.6 us (2%)
    pallas_call x1, Pallas kernels, factor(): pl.pallas_call(factor_kernel, out_shape=(jax.ShapeDtypeStruct((SUB_DEV, N...  21.2 us
    ppermute x8, starting transfers between devices, shifted(): lax.ppermute(value, ('row', 'col'), [(i, (i + amount) % size) for i in ra...  15 us
    pallas_call x1, Pallas kernels, assemble(): pl.pallas_call(assemble_kernel, out_shape=(jax.ShapeDtypeStruct((4, 3, NV...  11.6 us
    ppermute x2, starting transfers between devices, from_next(): return lax.ppermute(value, axis, pairs)  7.23 us
    ppermute x8, waiting for transfers between devices, shifted(): lax.ppermute(value, ('row', 'col'), [(i, (i + amount) % size) for i in ra...  7.09 us
    pallas_call x1, Pallas kernels, lateral(): pl.pallas_call(lateral_kernel, out_shape=(jax.ShapeDtypeStruct((SUB_DEV,...  3.39 us
    unnamed x20, local copies, waits for them, and re-layouts  2.22 us
    pallas_call x1, Pallas kernels, flatten(): pl.pallas_call(flatten_kernel, out_shape=(jax.ShapeDtypeStruct((7, SUB_DE...  1.94 us
  transfers between devices with their start and end apart: 10, of which 2 were waited for; matrix products, arithmetic and copies ran while one was open for 1% of the time, Pallas kernels for 18%

commit v1 on v0

--- a/solution.py
+++ b/solution.py
@@ -221,7 +221,7 @@
     return jnp.transpose(jnp.concatenate([block, jnp.zeros((80, 128), jnp.float32)], axis=0))[:NV]
 
 
-def lateral_kernel(order, ranks, below_x, below_y, main, own_x, own_y, roots_x, roots_y, blocks, share, side, plan, halo_x, halo_y):
+def lateral_kernel(order, ranks, below_x, below_y, main, own_x, own_y, roots_x, roots_y, blocks, share, side, plan, local, halo_x, halo_y):
     device = device_index()
     size = N_ROW * N_COL
     rank_all = ranks[...]
@@ -239,6 +239,7 @@
     plan[0] = device
     plan[1] = jnp.where(near, jnp.where(beside, offset + 3, jnp.where(from_below, 5, jnp.where(from_above, 6, 0))), 7)
     plan[2] = near.astype(jnp.int32)
+    local[0] = near.astype(jnp.int32)
     plan[3] = jnp.where(offset == 0, 0, jnp.where(offset == -1, 1, 2))
     for slot in range(12):
         plan[4 + slot] = (base * SUB_DEV + slot) & (SUBS - 1)
@@ -316,9 +317,10 @@
             jax.ShapeDtypeStruct((4, NV, 128), f32),
             jax.ShapeDtypeStruct((2, NV, 128), f32),
             jax.ShapeDtypeStruct((16,), jnp.int32),
+            jax.ShapeDtypeStruct((1,), jnp.int32),
         ),
         in_specs=[smem] + [vmem] * 8,
-        out_specs=(vmem, vmem, vmem, smem),
+        out_specs=(vmem, vmem, vmem, smem, smem),
         scratch_shapes=[
             pltpu.VMEM((4, 272, 128), f32),
             pltpu.VMEM((272, 128), f32),
@@ -778,7 +780,7 @@
     )(spot, right2, right1, share, left1, left2, side)
 
 
-def exchange(device, order, blocks, share, side, plan):
+def exchange(device, order, blocks, share, side, plan, local):
     subdomain = jnp.arange(SUBS, dtype=jnp.int32)
     my_order = lax.dynamic_slice(order, (device * SUB_DEV,), (SUB_DEV,))
 
@@ -819,7 +821,7 @@
         )
         return (whole.reshape(24, NV, 128), jnp.concatenate([plan[:4], listed]).astype(jnp.int32))
 
-    rescue, meta = lax.cond(plan[2] > 0, local_path, global_path, None)
+    rescue, meta = lax.cond(local.reshape(()) > 0, local_path, global_path, None)
     shares = (share, right1, right2, right3, left1, left2, left3)
     panel, flat = factor(order, meta, shares, below, above, rescue, blocks, high_y, flat)
     return (jnp.transpose(flat, (1, 0, 2)), panel)
@@ -865,8 +867,8 @@
     main, own_x, own_y, roots_x, roots_y = assemble(
         deflation, gradients.reshape(192, 64), coefficient, x_penalty, jnp.transpose(y_penalty, (1, 0, 2)), z_penalty
     )
-    blocks, share, side, plan = lateral(coarse_order, coarse_order.reshape(8, 128), below_x, below_y, main, own_x, own_y, roots_x, roots_y)
-    return exchange(device, coarse_order, blocks, share, side, plan)
+    blocks, share, side, plan, local = lateral(coarse_order, coarse_order.reshape(8, 128), below_x, below_y, main, own_x, own_y, roots_x, roots_y)
+    return exchange(device, coarse_order, blocks, share, side, plan, local)
 
 
 def solution(mesh):

time: 75.1 us -> 76.4 us (1.017)
  the two profiles are of different devices: /device:TPU:3 before, /device:TPU:0 now
where the time goes in v1:
time: 76.4 us; the launch traced here: 77.3 us
  Pallas kernels  41.8 us (55%)
  starting transfers between devices  24.5 us (32%)
  waiting for transfers between devices  6.91 us (9%)
  local copies, waits for them, and re-layouts  2.26 us (3%)
  between operations  1.63 us (2%)
    pallas_call x1, Pallas kernels, factor(): pl.pallas_call(factor_kernel, out_shape=(jax.ShapeDtypeStruct((SUB_DEV, N...  21.2 us
    ppermute x8, starting transfers between devices, shifted(): lax.ppermute(value, ('row', 'col'), [(i, (i + amount) % size) for i in ra...  20.7 us
    pallas_call x1, Pallas kernels, assemble(): pl.pallas_call(assemble_kernel, out_shape=(jax.ShapeDtypeStruct((4, 3, NV...  11.6 us
    ppermute x8, waiting for transfers between devices, shifted(): lax.ppermute(value, ('row', 'col'), [(i, (i + amount) % size) for i in ra...  6.9 us
    ppermute x2, starting transfers between devices, from_next(): return lax.ppermute(value, axis, pairs)  3.88 us
    pallas_call x1, Pallas kernels, lateral(): pl.pallas_call(lateral_kernel, out_shape=(jax.ShapeDtypeStruct((SUB_DEV,...  3.39 us
    unnamed x20, local copies, waits for them, and re-layouts  2.22 us
    pallas_call x1, Pallas kernels, flatten(): pl.pallas_call(flatten_kernel, out_shape=(jax.ShapeDtypeStruct((7, SUB_DE...  1.94 us
  transfers between devices with their start and end apart: 10, of which 3 were waited for; matrix products, arithmetic and copies ran while one was open for 0% of the time, Pallas kernels for 17%

profile of v1, /device:TPU:0, one launch (start us, length us, event | category | flops | bytes accessed | tf_op | source)
XLA Modules:
  0.0 77.3 jit_solution(2986116847117715007)
XLA Ops:
  0.6 1.8 %edges.1 = (bf16[8,16,768]{2,1,0:T(8,128)(2,1)}, bf16[2,16,3072]{2,1,0:T(8,128)(2,1)}) custom-call(bf16[2,8,16,3072]{3,2,1,0:T(8,128)(2,1)} %deflation.3), custom_call_target="tpu_custom_call" | custom-call | tf_op jit(solution)/shard_map/edges/pallas_call | solution.py:843
  2.4 1.3 %collective-permute-start.8 = (bf16[8,16,768]{2,1,0:T(8,128)(2,1)}, bf16[8,16,768]{2,1,0:T(8,128)(2,1)S(1)}, u32[]{:S(2)}, u32[]{:S(2)}) collective-permute-start(bf16[8,16,768]{2,1,0:T(8,128)(2,1)} %get-tuple-element.39), channel_id=1, source_target_pairs={{0,32},{32,64},{64,96},{96,128},{128,160},{160,192},{192,224},{1,3... | collective-permute-start | bytes 589832 | tf_op jit(solution)/shard_map/ppermute | solution.py:859
  3.7 2.6 %collective-permute-start.9 = (bf16[2,16,3072]{2,1,0:T(8,128)(2,1)}, bf16[2,16,3072]{2,1,0:T(8,128)(2,1)S(1)}, u32[]{:S(2)}, u32[]{:S(2)}) collective-permute-start(bf16[2,16,3072]{2,1,0:T(8,128)(2,1)} %get-tuple-element.40), channel_id=1, source_target_pairs={{0,1},{1,2},{2,3},{3,4},{4,5},{5,6},{6,7},{7,8},{8,9},{9,10},{10,1... | collective-permute-start | bytes 589832 | tf_op jit(solution)/shard_map/ppermute | solution.py:859
  6.3 0.0 copy-start.6
  6.3 11.6 %assemble.1 = (f32[4,3,48,128]{3,2,1,0:T(8,128)}, bf16[4,256,128]{2,1,0:T(8,128)(2,1)}, bf16[256,128]{1,0:T(8,128)(2,1)}, f32[4,16,128]{2,1,0:T(8,128)}, f32[16,128]{1,0:T(8,128)}) custom-call(bf16[2,8,16,3072]{3,2,1,0:T(8,128)(2,1)} %deflation.3, bf16[192,64]{1,0:T(8,128)(2,1)} %bitcast.61, f32[2,8,16]{2,1,0:T(8,128)} %coefficient.1, ...), custom_call_target="tpu_custom_call" | custom-call | flops 2000000000 | bytes 3000000 | tf_op jit(solution)/shard_map/assemble/pallas_call | solution.py:189
  17.9 0.0 collective-permute-done.8.below_x
  17.9 0.0 copy-start.7
  17.9 0.0 collective-permute-done.9.below_y
  18.0 0.6 copy-done.7
  18.6 0.1 copy-done.8
  18.7 3.4 %lateral.1 = (f32[4,5,48,128]{3,2,1,0:T(8,128)S(1)}, f32[4,48,128]{2,1,0:T(8,128)}, f32[2,48,128]{2,1,0:T(8,128)}, s32[16]{0:T(128)S(1)}, s32[1]{0:T(128)}) custom-call(s32[1024]{0:T(1024)S(1)} %copy-done.6, s32[8,128]{1,0:T(8,128)S(1)} %bitcast.59, bf16[8,16,768]{2,1,0:T(8,128)(2,1)} %copy-done.7, bf16[2,16,3072]{2,1,0:T(8,128)(2,1)} %copy-done.8, ...), custom_call_target="tpu_custom_call" | custom-call | tf_op jit(solution)/shard_map/lateral/pallas_call | solution.py:313
  22.1 2.0 %collective-permute-start.10 = (f32[4,48,128]{2,1,0:T(8,128)}, f32[4,48,128]{2,1,0:T(8,128)S(1)}, u32[]{:S(2)}, u32[]{:S(2)}) collective-permute-start(f32[4,48,128]{2,1,0:T(8,128)} %get-tuple-element.50.share.own), channel_id=1, source_target_pairs={{0,1},{1,2},{2,3},{3,4},{4,5},{5,6},{6,7},{7,8},{8,9},{9,10},{10,1... | collective-permute-start | bytes 294920 | tf_op jit(solution)/shard_map/ppermute | solution.py:745
  24.1 4.5 %collective-permute-start.11 = (f32[4,48,128]{2,1,0:T(8,128)}, f32[4,48,128]{2,1,0:T(8,128)S(1)}, u32[]{:S(2)}, u32[]{:S(2)}) collective-permute-start(f32[4,48,128]{2,1,0:T(8,128)} %get-tuple-element.50.share.own), channel_id=1, source_target_pairs={{0,2},{1,3},{2,4},{3,5},{4,6},{5,7},{6,8},{7,9},{8,10},{9,11},{10,... | collective-permute-start | bytes 294920 | tf_op jit(solution)/shard_map/ppermute | solution.py:745
  28.5 4.0 %collective-permute-start.13 = (f32[4,48,128]{2,1,0:T(8,128)}, f32[4,48,128]{2,1,0:T(8,128)S(1)}, u32[]{:S(2)}, u32[]{:S(2)}) collective-permute-start(f32[4,48,128]{2,1,0:T(8,128)} %get-tuple-element.50.share.own), channel_id=1, source_target_pairs={{0,255},{1,0},{2,1},{3,2},{4,3},{5,4},{6,5},{7,6},{8,7},{9,8},{10,... | collective-permute-start | bytes 294920 | tf_op jit(solution)/shard_map/ppermute | solution.py:745
  32.6 3.1 %collective-permute-done.11.right2 = f32[4,48,128]{2,1,0:T(8,128)S(1)} collective-permute-done((f32[4,48,128]{2,1,0:T(8,128)}, f32[4,48,128]{2,1,0:T(8,128)S(1)}, u32[]{:S(2)}, u32[]{:S(2)}) %collective-permute-start.11) | collective-permute-done | bytes 98336 | tf_op jit(solution)/shard_map/ppermute | solution.py:745
  35.7 1.9 %collective-permute-done.13.left1.above = f32[4,48,128]{2,1,0:T(8,128)S(1)} collective-permute-done((f32[4,48,128]{2,1,0:T(8,128)}, f32[4,48,128]{2,1,0:T(8,128)S(1)}, u32[]{:S(2)}, u32[]{:S(2)}) %collective-permute-start.13) | collective-permute-done | bytes 98336 | tf_op jit(solution)/shard_map/ppermute | solution.py:745
  37.7 1.8 %collective-permute-done.14.left2 = f32[4,48,128]{2,1,0:T(8,128)S(1)} collective-permute-done((f32[4,48,128]{2,1,0:T(8,128)}, f32[4,48,128]{2,1,0:T(8,128)S(1)}, u32[]{:S(2)}, u32[]{:S(2)}) %collective-permute-start.14) | collective-permute-done | bytes 98336 | tf_op jit(solution)/shard_map/ppermute | solution.py:745
  39.5 0.6 copy-done.3
  40.1 1.9 %choose.1 = f32[14,48,128]{2,1,0:T(8,128)} custom-call(s32[16]{0:T(128)S(1)} %get-tuple-element.48.spot, f32[4,48,128]{2,1,0:T(8,128)} %copy-done.2, f32[4,48,128]{2,1,0:T(8,128)} %copy-done.1, f32[4,48,128]{2,1,0:T(8,128)} %get-tuple-element.50.share.own, f32[4,48,128]{2,1,0:T(8,128)} %copy-done, f32[4,48,128]{2,1,0:T(8,128)} %copy-done.3, ...), custom_call_target="tpu_custom_call" | custom-call | tf_op jit(solution)/shard_map/choose/pallas_call | solution.py:774
  42.0 0.0 collective-permute-start.16
  42.0 2.9 %collective-permute-start.17 = (f32[14,48,128]{2,1,0:T(8,128)}, f32[14,48,128]{2,1,0:T(8,128)S(1)}, u32[]{:S(2)}, u32[]{:S(2)}) collective-permute-start(f32[14,48,128]{2,1,0:T(8,128)} %choose.1), channel_id=1, source_target_pairs={{0,224},{1,225},{2,226},{3,227},{4,228},{5,229},{6,230},{7,231},{8... | collective-permute-start | bytes 1032200 | tf_op jit(solution)/shard_map/ppermute | solution.py:745
  45.0 7.2 %collective-permute-start.15 = (f32[4,48,128]{2,1,0:T(8,128)}, f32[4,48,128]{2,1,0:T(8,128)}, u32[]{:S(2)}, u32[]{:S(2)}) collective-permute-start(f32[4,48,128]{2,1,0:T(8,128)} %copy-done.3), channel_id=1, source_target_pairs={{0,255},{1,0},{2,1},{3,2},{4,3},{5,4},{6,5},{7,6},{8,7},{9,8},{10,... | collective-permute-start | bytes 294920 | tf_op jit(solution)/shard_map/ppermute | solution.py:745
  52.8 0.3 conditional.1
  53.1 1.9 %flatten.1 = (f32[7,4,2304]{2,1,0:T(4,128)}, f32[4,48,128]{2,1,0:T(8,128)}) custom-call(s32[1024]{0:T(1024)S(1)} %copy-done.6, f32[4,5,48,128]{3,2,1,0:T(8,128)S(1)} %get-tuple-element.47.blocks, f32[4,48,128]{2,1,0:T(8,128)} %copy-done), custom_call_target="tpu_custom_call" | custom-call | flops 1000000 | bytes 2000000 | tf_op jit(solution)/shard_map/flatten/pallas_call | solution.py:377
  55.1 0.0 collective-permute-done.12.right3
  55.1 0.0 collective-permute-done.15.left3
  55.1 0.0 collective-permute-done.16.below
  55.1 0.0 collective-permute-done.17.above
  55.1 0.6 copy-done.9
  55.7 0.2 copy-done.4
  55.9 0.1 copy-done.5
  56.0 21.2 %factor.1 = (f32[4,48,528]{2,1,0:T(8,128)}, f32[7,4,2304]{2,1,0:T(4,128)}) custom-call(s32[1024]{0:T(1024)S(1)} %copy-done.6, s32[16]{0:T(128)S(1)} %get-tuple-element.49.meta, f32[4,48,128]{2,1,0:T(8,128)} %get-tuple-element.50.share.own, f32[4,48,128]{2,1,0:T(8,128)} %copy-done.1, f32[4,48,128]{2,1,0:T(8,128)} %copy-done.2, ...), custom_call_target="tpu_custom_call", output_to_operand_aliasing={{1}: (14, {})} | custom-call | tf_op jit(solution)/shard_map/factor/pallas_call | solution.py:716
  (17 shorter events, 0.1 us)
Async XLA Ops:
  2.4 15.5 %collective-permute-start.8 = (bf16[8,16,768]{2,1,0:T(8,128)(2,1)}, bf16[8,16,768]{2,1,0:T(8,128)(2,1)S(1)}, u32[]{:S(2)}, u32[]{:S(2)}) collective-permute-start(bf16[8,16,768]{2,1,0:T(8,128)(2,1)} %get-tuple-element.39), channel_id=1, source_target_pairs={{0,32},{32,64},{64,96},{96,128},{128,160},{160,192},{192,224},{1,3... | collective-permute-start | bytes 589832 | tf_op jit(solution)/shard_map/ppermute | solution.py:859
  3.7 14.2 %collective-permute-start.9 = (bf16[2,16,3072]{2,1,0:T(8,128)(2,1)}, bf16[2,16,3072]{2,1,0:T(8,128)(2,1)S(1)}, u32[]{:S(2)}, u32[]{:S(2)}) collective-permute-start(bf16[2,16,3072]{2,1,0:T(8,128)(2,1)} %get-tuple-element.40), channel_id=1, source_target_pairs={{0,1},{1,2},{2,3},{3,4},{4,5},{5,6},{6,7},{7,8},{8,9},{9,10},{10,1... | collective-permute-start | bytes 589832 | tf_op jit(solution)/shard_map/ppermute | solution.py:859
  6.3 12.3 %copy-start.6 = (s32[1024]{0:T(1024)S(1)}, s32[1024]{0:T(1024)}, u32[]{:S(2)}) copy-start(s32[1024]{0:T(1024)} %order.5) | copy-start | bytes 12292
  17.9 0.7 copy-start.7
  17.9 0.7 copy-start.8
  22.1 10.5 %collective-permute-start.10 = (f32[4,48,128]{2,1,0:T(8,128)}, f32[4,48,128]{2,1,0:T(8,128)S(1)}, u32[]{:S(2)}, u32[]{:S(2)}) collective-permute-start(f32[4,48,128]{2,1,0:T(8,128)} %get-tuple-element.50.share.own), channel_id=1, source_target_pairs={{0,1},{1,2},{2,3},{3,4},{4,5},{5,6},{6,7},{7,8},{8,9},{9,10},{10,1... | collective-permute-start | bytes 294920 | tf_op jit(solution)/shard_map/ppermute | solution.py:745
  24.1 11.7 %collective-permute-start.11 = (f32[4,48,128]{2,1,0:T(8,128)}, f32[4,48,128]{2,1,0:T(8,128)S(1)}, u32[]{:S(2)}, u32[]{:S(2)}) collective-permute-start(f32[4,48,128]{2,1,0:T(8,128)} %get-tuple-element.50.share.own), channel_id=1, source_target_pairs={{0,2},{1,3},{2,4},{3,5},{4,6},{5,7},{6,8},{7,9},{8,10},{9,11},{10,... | collective-permute-start | bytes 294920 | tf_op jit(solution)/shard_map/ppermute | solution.py:745
  28.5 9.1 %collective-permute-start.13 = (f32[4,48,128]{2,1,0:T(8,128)}, f32[4,48,128]{2,1,0:T(8,128)S(1)}, u32[]{:S(2)}, u32[]{:S(2)}) collective-permute-start(f32[4,48,128]{2,1,0:T(8,128)} %get-tuple-element.50.share.own), channel_id=1, source_target_pairs={{0,255},{1,0},{2,1},{3,2},{4,3},{5,4},{6,5},{7,6},{8,7},{9,8},{10,... | collective-permute-start | bytes 294920 | tf_op jit(solution)/shard_map/ppermute | solution.py:745
  32.6 6.9 %collective-permute-start.14 = (f32[4,48,128]{2,1,0:T(8,128)}, f32[4,48,128]{2,1,0:T(8,128)S(1)}, u32[]{:S(2)}, u32[]{:S(2)}) collective-permute-start(f32[4,48,128]{2,1,0:T(8,128)} %get-tuple-element.50.share.own), channel_id=1, source_target_pairs={{0,254},{1,255},{2,0},{3,1},{4,2},{5,3},{6,4},{7,5},{8,6},{9,7},{1... | collective-permute-start | bytes 294920 | tf_op jit(solution)/shard_map/ppermute | solution.py:745
  32.6 6.9 %copy-start.1 = (f32[4,48,128]{2,1,0:T(8,128)}, f32[4,48,128]{2,1,0:T(8,128)S(1)}, u32[]{:S(2)}) copy-start(f32[4,48,128]{2,1,0:T(8,128)S(1)} %collective-permute-done.10.right1) | copy-start | bytes 294916
  35.7 3.8 %copy-start.2 = (f32[4,48,128]{2,1,0:T(8,128)}, f32[4,48,128]{2,1,0:T(8,128)S(1)}, u32[]{:S(2)}) copy-start(f32[4,48,128]{2,1,0:T(8,128)S(1)} %collective-permute-done.11.right2) | copy-start | bytes 294916
  37.7 1.8 %copy-start = (f32[4,48,128]{2,1,0:T(8,128)}, f32[4,48,128]{2,1,0:T(8,128)S(1)}, u32[]{:S(2)}) copy-start(f32[4,48,128]{2,1,0:T(8,128)S(1)} %collective-permute-done.13.left1.above) | copy-start | bytes 294916
  39.5 0.6 copy-start.3
  42.0 13.1 %collective-permute-start.16 = (f32[14,48,128]{2,1,0:T(8,128)}, f32[14,48,128]{2,1,0:T(8,128)S(1)}, u32[]{:S(2)}, u32[]{:S(2)}) collective-permute-start(f32[14,48,128]{2,1,0:T(8,128)} %choose.1), channel_id=1, source_target_pairs={{0,32},{1,33},{2,34},{3,35},{4,36},{5,37},{6,38},{7,39},{8,40},{9,... | collective-permute-start | bytes 1032200 | tf_op jit(solution)/shard_map/ppermute | solution.py:745
  42.0 13.1 %collective-permute-start.17 = (f32[14,48,128]{2,1,0:T(8,128)}, f32[14,48,128]{2,1,0:T(8,128)S(1)}, u32[]{:S(2)}, u32[]{:S(2)}) collective-permute-start(f32[14,48,128]{2,1,0:T(8,128)} %choose.1), channel_id=1, source_target_pairs={{0,224},{1,225},{2,226},{3,227},{4,228},{5,229},{6,230},{7,231},{8... | collective-permute-start | bytes 1032200 | tf_op jit(solution)/shard_map/ppermute | solution.py:745
  45.0 10.1 %collective-permute-start.12 = (f32[4,48,128]{2,1,0:T(8,128)}, f32[4,48,128]{2,1,0:T(8,128)S(1)}, u32[]{:S(2)}, u32[]{:S(2)}) collective-permute-start(f32[4,48,128]{2,1,0:T(8,128)} %copy-done.2), channel_id=1, source_target_pairs={{0,1},{1,2},{2,3},{3,4},{4,5},{5,6},{6,7},{7,8},{8,9},{9,10},{10,1... | collective-permute-start | bytes 294920 | tf_op jit(solution)/shard_map/ppermute | solution.py:745
  45.0 10.1 %collective-permute-start.15 = (f32[4,48,128]{2,1,0:T(8,128)}, f32[4,48,128]{2,1,0:T(8,128)}, u32[]{:S(2)}, u32[]{:S(2)}) collective-permute-start(f32[4,48,128]{2,1,0:T(8,128)} %copy-done.3), channel_id=1, source_target_pairs={{0,255},{1,0},{2,1},{3,2},{4,3},{5,4},{6,5},{7,6},{8,7},{9,8},{10,... | collective-permute-start | bytes 294920 | tf_op jit(solution)/shard_map/ppermute | solution.py:745
  55.1 0.6 copy-start.9
  55.1 0.8 %copy-start.4 = (f32[14,48,128]{2,1,0:T(8,128)}, f32[14,48,128]{2,1,0:T(8,128)S(1)}, u32[]{:S(2)}) copy-start(f32[14,48,128]{2,1,0:T(8,128)S(1)} %collective-permute-done.16.below) | copy-start | bytes 1032196
  55.1 0.9 %copy-start.5 = (f32[14,48,128]{2,1,0:T(8,128)}, f32[14,48,128]{2,1,0:T(8,128)S(1)}, u32[]{:S(2)}) copy-start(f32[14,48,128]{2,1,0:T(8,128)S(1)} %collective-permute-done.17.above) | copy-start | bytes 1032196
